TPU v7x, 512 devices: a whole 4x4x16 slice. The times are simulated.
512 devices in a mesh: grp: 16 (over y, z_hi, core), sub: 32 (over x, z_lo).
Axes of the slice: x: 4, y: 4, z: 16 (z_hi: 2, z_lo: 8; z = z_hi * 8 + z_lo), core: 2. Of those that a mesh axis runs over, the one named last changes fastest.
Arguments:
- activations: bfloat16 [262144, 2048], P(('grp', 'sub')), may hold values from -110 to 110
- norm_gain: float32 [2048], replicated, may hold values from 0.5 to 1.5
- key_weight: bfloat16 [2048, 768], P('sub'), may hold values from -0.125 to 0.125
- key_grads: bfloat16 [262144, 768], P(('grp', 'sub')), may hold values from -3 to 3
Outputs:
- input_grads: bfloat16 [262144, 2048], P(('grp', 'sub'))
- weight_grads: float32 [2048, 768], P('sub', 'grp')
- gain_grads: float32 [2048], P('sub')
All inputs are finite; a program needn't handle non-finite values.
Results may differ from a plain program's by a relative error of at most 0.0029.
Values may be sent and summed in bfloat16 or wider, within the bound.
A program may use at most 64 MiB of HBM per device.

v0:
```python
import jax
import jax.numpy as jnp
from jax import lax
from jax.sharding import PartitionSpec as P


def local(activations, norm_gain, key_weight, key_grads):
    inputs = activations.astype(jnp.float32)
    mean_square = jnp.mean(inputs * inputs, axis=1, keepdims=True)
    inverse_rms = lax.rsqrt(mean_square + 1e-05)
    normed = inputs * inverse_rms
    scaled = (normed * norm_gain).astype(jnp.bfloat16)
    grad_scaled = lax.dot_general(
        key_grads,
        lax.all_gather(key_weight, "sub", axis=0, tiled=True),
        (((1,), (1,)), ((), ())),
        preferred_element_type=jnp.float32,
    )
    gained = norm_gain * grad_scaled
    input_grads = (
        inverse_rms * (gained - normed * jnp.mean(gained * normed, axis=1, keepdims=True))
    ).astype(jnp.bfloat16)
    groups = lax.axis_size("grp")
    members = lax.axis_size("sub")
    feature_rows = key_weight.shape[0]
    key_width = key_grads.shape[1]
    term = lax.dot_general(
        scaled, key_grads, (((0,), (0,)), ((), ())), preferred_element_type=jnp.float32
    )
    received = lax.all_to_all(term, "sub", split_axis=0, concat_axis=1, tiled=True)
    shared = jnp.sum(received.reshape(feature_rows, members, key_width), axis=1)
    owned = lax.psum_scatter(shared, "grp", scatter_dimension=1, tiled=True)
    weight_grads = owned / groups
    local_gain = jnp.sum(grad_scaled * normed, axis=0)
    summed = lax.psum(local_gain, ("grp", "sub"))
    gain_sum = lax.dynamic_slice_in_dim(summed, lax.axis_index("sub") * feature_rows, feature_rows)
    gain_grads = gain_sum / groups
    return (input_grads, weight_grads, gain_grads)


def solution(mesh):
    return jax.shard_map(
        local,
        mesh=mesh,
        in_specs=(P(("grp", "sub"), None), P(), P("sub", None), P(("grp", "sub"), None)),
        out_specs=(P(("grp", "sub"), None), P("sub", "grp"), P("sub")),
        check_vma=False,
    )
```

profile of v0, /device:TPU:1, one launch (start us, length us, event | category | flops | bytes accessed | tf_op | source)
XLA Modules:
  0.0 569.3 jit_solution(18334966130599238533)
XLA Ops:
  8.0 0.0 copy-start
  8.0 2.1 fusion.10
  10.2 0.0 copy-done
  10.2 6.2 %fusion.11 = f32[2048,768]{1,0:T(8,128)} fusion(bf16[512,768]{1,0:T(8,128)(2,1)S(1)} %copy-done, bf16[512,2048]{1,0:T(8,128)(2,1)} %param.4, f32[2048]{0:T(1024)} %param.5, f32[512]{0:T(512)S(1)} %add_rsqrt_fusion), kind=kOutput, calls=%fused_computation.13 | convolution fusion | flops 1614807040 | bytes 9185280 | tf_op jit(solution)/shard_map/dot_general | solution.py:27
  16.4 0.0 copy-start.1
  16.4 0.0 copy-start.2
  16.4 16.2 %all-to-all-start = ((f32[32,64,768]{2,1,0:T(8,128)}), f32[32,64,768]{2,1,0:T(8,128)}, u32[]{:S(2)}, u32[]{:S(2)}) async-start(f32[32,64,768]{2,1,0:T(8,128)} %bitcast.6), calls=%async_computation | async-start | bytes 12582912 | tf_op jit(solution)/shard_map/all_to_all | solution.py:30
  32.5 0.0 all-gather.2.cloned.1.call-start
  32.6 0.7 all-gather.2.cloned.1.call-update
  33.3 0.0 reduce-scatter.4.cloned.1.call-start
  33.3 391.8 %all-gather.2.cloned.1.call-done = bf16[2048,768]{1,0:T(8,128)(2,1)} async-done(((bf16[64,768]{1,0:T(8,128)(2,1)}), bf16[2048,768]{1,0:T(8,128)(2,1)}) %all-gather.2.cloned.1.call-update) | async-done | bytes 3145744 | tf_op jit(solution)/shard_map/all_gather | solution.py:15
  425.2 0.0 copy-done.1
  425.2 0.0 copy-done.2
  425.2 6.0 %fusion.9 = (f32[2048]{0:T(1024)S(1)}, f32[512]{0:T(512)S(1)}, f32[512,2048]{1,0:T(8,128)}) fusion(bf16[512,2048]{1,0:T(8,128)(2,1)S(1)} %copy-done.1, f32[512]{0:T(512)S(1)} %add_rsqrt_fusion, f32[2048]{0:T(1024)S(1)} %copy-done.2, bf16[512,768]{1,0:T(8,128)(2,1)S(1)} %copy-done, bf16[2048,768]{1,0:T(8,128)(2,1)} %all-gather.2.cloned.1.call-done), kind=kOutput, calls=%fused_computation.11 | convolution fusion | flops 1617950208 | bytes 10244096 | tf_op jit(solution)/shard_map/dot_general | solution.py:13
  431.1 0.0 all-to-all-done
  431.1 3.1 reduce_sum.38
  434.2 0.9 copy.9
  435.1 0.0 reduce-scatter.4.cloned.1.call-update
  435.2 4.6 fusion.7
  439.7 120.0 %psum.7 = f32[2048]{0:T(1024)S(1)} all-reduce(f32[2048]{0:T(1024)S(1)} %get-tuple-element.9), channel_id=1, replica_groups=mesh['grp'=16,'sub'=32] {'grp','sub'}, use_global_device_ids=true, to_apply=%region_5.0 | all-reduce | flops 2048 | bytes 16384 | tf_op jit(solution)/shard_map/psum | solution.py:35
  559.8 0.6 dynamic-slice_multiply_fusion
  560.4 0.0 reduce-scatter.4.cloned.1.call-done
  560.4 0.8 copy.10
  561.2 0.7 copy.8
  (3 shorter events, 0.0 us)
Async XLA Ops:
  8.0 2.2 copy-start
  16.4 408.8 %copy-start.1 = (bf16[512,2048]{1,0:T(8,128)(2,1)S(1)}, bf16[512,2048]{1,0:T(8,128)(2,1)}, u32[]{:S(2)}) copy-start(bf16[512,2048]{1,0:T(8,128)(2,1)} %param.4) | copy-start | bytes 6291460
  16.4 408.8 %copy-start.2 = (f32[2048]{0:T(1024)S(1)}, f32[2048]{0:T(1024)}, u32[]{:S(2)}) copy-start(f32[2048]{0:T(1024)} %param.5) | copy-start | bytes 24580
  16.4 414.7 %all-to-all-start = ((f32[32,64,768]{2,1,0:T(8,128)}), f32[32,64,768]{2,1,0:T(8,128)}, u32[]{:S(2)}, u32[]{:S(2)}) async-start(f32[32,64,768]{2,1,0:T(8,128)} %bitcast.6), calls=%async_computation | async-start | bytes 12582912 | tf_op jit(solution)/shard_map/all_to_all | solution.py:30
  32.5 392.6 %all-gather.2.cloned.1.call-start = ((), (), s32[]{:S(2)}) async-start(), calls=%async_computation.2 | async-start | bytes 3244032 | tf_op jit(solution)/shard_map/all_gather | solution.py:15
  33.3 527.1 %reduce-scatter.4.cloned.1.call-start = ((), (), s32[]{:S(2)}) async-start(), calls=%async_computation.3 | async-start | bytes 417792
Sparse Core Ops, SparseCore 0:
  35.4 389.6 all-gather.1
Sparse Core Ops, SparseCore 1:
  435.2 108.9 reduce-scatter.3
where the time goes:
time: 570 us; the launch traced here: 569 us
  waiting for transfers between devices  393 us (69%)
  blocking collectives  120 us (21%)
  starting transfers between devices  16.2 us (3%)
  between operations  15.5 us (3%)
  matrix products  12.1 us (2%)
  other arithmetic  10.4 us (2%)
    all_gather x1, waiting for transfers between devices, local(): lax.all_gather(key_weight, 'sub', axis=0, tiled=True)  392 us
    psum x1, blocking collectives, local(): summed = lax.psum(local_gain, ('grp', 'sub'))  120 us
    all_to_all x1, starting transfers between devices, local(): lax.all_to_all(term, 'sub', split_axis=0, concat_axis=1, tiled=True)  16.2 us
  transfers between devices with their start and end apart: 3, of which 1 were waited for; matrix products, arithmetic and copies ran while one was open for 2% of the time, Pallas kernels for 0%

commit v1 on v0

v1 whole, which is shorter than its diff:
```python
import functools

import jax
import jax.numpy as jnp
from jax import lax
from jax.experimental import pallas as pl
from jax.experimental.pallas import tpu as pltpu
from jax.sharding import PartitionSpec as P

MESH = pl.DeviceIdType.MESH
F32 = jnp.float32
BF16 = jnp.bfloat16
NX, NY, NZL, NZH = 4, 4, 8, 2
NZ = NZL * NZH
ORDER = (0, 1, 3, 2)


def kernel(
    act, gain, weight, grads,
    out, tail,
    scaled, inv, grads_t, w, t32, p_send, p_recv, p, rs_a, rs_b, rs_c, rs_d, rs_e, rs_f, q, u, u_send, u_recv,
    v, z_send, z_recv, lg, g_own, g_part, g_x, g_y,
    send, agz, ag1, ag2l, ag2r, agfl, agfr, agp, rsp, rs1, rs2, zsem, gp, gx, gy,
):
    g_idx, s_idx = lax.axis_index("grp"), lax.axis_index("sub")
    core = lax.rem(g_idx, 2)
    zh = lax.rem(lax.div(g_idx, 2), 2)
    y = lax.div(g_idx, 4)
    x = lax.div(s_idx, NZL)
    zl = lax.rem(s_idx, NZL)
    z = zh * NZL + zl
    f = x + core * (y - x)
    s = y + core * (x - y)
    tokens, model = act.shape
    key = grads.shape[1]

    def dev(dx, dy, dz, dc):
        return ((dy * 2 + lax.div(dz, NZL)) * 2 + dc, dx * NZL + lax.rem(dz, NZL))

    def xy(df, ds):
        return df + core * (ds - df), ds + core * (df - ds)

    def dev_fs(df, ds):
        dx, dy = xy(df, ds)
        return dev(dx, dy, z, core)

    def m4(a):
        return lax.rem(a, 4)

    partner = dev(x, y, z, 1 - core)
    right, left = m4(f + 1), m4(f + 3)
    s_right, s_left = m4(s + 1), m4(s + 3)

    sent = []

    def copy(src, dst, recv, device):
        return pltpu.make_async_remote_copy(
            src_ref=src, dst_ref=dst, send_sem=send.at[len(sent)], recv_sem=recv,
            device_id=device, device_id_type=MESH,
        )

    def go(src, dst, recv, device):
        made = copy(src, dst, recv, device)
        made.start()
        sent.append(made)

    def got(dst, recv, device):
        pltpu.make_async_remote_copy(
            src_ref=dst, dst_ref=dst, send_sem=send.at[0], recv_sem=recv,
            device_id=device, device_id_type=MESH,
        ).wait_recv()

    barrier = pltpu.get_barrier_semaphore()
    peers = [partner]
    peers += [dev(m4(x + k), y, z, core) for k in range(1, NX)]
    peers += [dev(x, m4(y + k), z, core) for k in range(1, NY)]
    peers += [dev(x, y, lax.rem(z + k, NZ), core) for k in range(1, NZ)]
    for peer in peers:
        pl.semaphore_signal(barrier, inc=1, device_id=peer, device_id_type=MESH)

    rows = 64

    @pl.loop(0, tokens // rows)
    def _(i):
        block = pl.ds(pl.multiple_of(i * rows, rows), rows)
        a = act[block, :].astype(F32)
        r = lax.rsqrt(jnp.sum(a * a, axis=1, keepdims=True) * (1.0 / model) + 1e-05)
        inv[block, :] = jnp.broadcast_to(r, (rows, 128))
        scaled[block, :] = (a * r * gain[...]).astype(BF16)

    grads_t[...] = grads[...].T.reshape(16, 48, tokens)

    pl.semaphore_wait(barrier, len(peers))

    half = 4 * core
    mine = lax.div(zl, 4) == core
    z_offsets = (1, 15, 2, 14, 3, 13, 4)

    @pl.when(mine)
    def _():
        w[x, zl, y] = weight[y]

    def z_copy(n, off):
        return pltpu.make_async_remote_copy(
            src_ref=weight.at[y], dst_ref=w.at[x, zl, y],
            send_sem=send.at[n], recv_sem=agz.at[lax.rem(zl, 4)],
            device_id=dev(x, y, lax.rem(z + off, NZ), core), device_id_type=MESH,
        )

    @pl.when(mine)
    def _():
        for n, off in enumerate(z_offsets):
            z_copy(n, off).start()

    sent.extend([None] * len(z_offsets))

    def product(parity, i):
        lhs = jnp.concatenate([grads_t[2 * j + parity] for j in range(8)], axis=0)
        rhs = scaled[:, pl.ds(pl.multiple_of(i * 512, 512), 512)]
        return jnp.dot(lhs, rhs, preferred_element_type=F32).reshape(8, 48, 512)

    first = len(sent)

    def p_copy(i):
        return pltpu.make_async_remote_copy(
            src_ref=p_send.at[i], dst_ref=p_recv.at[i], send_sem=send.at[first + i],
            recv_sem=rsp.at[i], device_id=partner, device_id_type=MESH,
        )

    @pl.loop(0, NX)
    def _(i):
        p_send[i] = product(1 - core, i).astype(BF16)
        p_copy(i).start()

    sent.extend(p_copy(i) for i in range(NX))

    @pl.loop(0, NX)
    def _(i):
        t32[i] = product(core, i)

    def piece(df, ds):
        dx, dy = xy(df, ds)
        return w.at[dx, pl.ds(half, 4), dy]

    def pass_on(k, ds):
        at = piece(m4(f + k), ds)
        go(at, at, agp, partner)

    def spread(k):
        at = piece(m4(f + k), s)
        go(at, at, ag2l.at[k], dev_fs(f, s_right))
        go(at, at, ag2r.at[k], dev_fs(f, s_left))

    for i in range(4):
        @pl.when(half + i != zl)
        def _():
            got(w.at[x, half + i, y], agz.at[i], partner)

    own = piece(f, s)
    for k in (1, 3, 2):
        go(own, own, ag1.at[4 - k], dev_fs(m4(f + k), s))
    spread(0)
    pass_on(0, s)

    @pl.loop(0, NX)
    def _(i):
        p_copy(i).wait_recv()
        for dy in range(NY):
            df, ds = xy(i, dy)
            for dz in range(NZH):
                total = t32[i, 2 * dy + dz] + p_recv[i, 2 * dy + dz].astype(F32)
                t32[i, 2 * dy + dz] = total
                p[df, ds, dz] = total.astype(BF16)

    for k in (1, 3, 2):
        got(piece(m4(f + k), s), ag1.at[k], dev_fs(m4(f + k), s))
        spread(k)
        pass_on(k, s)

    def part(df, h):
        return p.at[m4(df), pl.ds(2 * h, 2)]

    to_right, to_left = dev_fs(right, s), dev_fs(left, s)
    go(part(f + 2, 0), rs_a, rs1.at[0], to_right)
    go(part(f + 2, 1), rs_c, rs1.at[2], to_left)
    go(part(f + 1, 1), rs_b, rs1.at[1], to_right)
    go(part(f + 3, 0), rs_d, rs1.at[3], to_left)

    for k in ORDER:
        got(piece(m4(f + k), s_left), ag2l.at[k], dev_fs(f, s_left))
        if k in ORDER[:2]:
            at = piece(m4(f + k), s_left)
            go(at, at, agfl.at[k], dev_fs(f, s_right))
        pass_on(k, s_left)
        got(piece(m4(f + k), s_right), ag2r.at[k], dev_fs(f, s_right))
        if k in ORDER[2:]:
            at = piece(m4(f + k), s_right)
            go(at, at, agfr.at[k], dev_fs(f, s_left))
        pass_on(k, s_right)

    def term(df, ds, dz):
        dx, dy = xy(df, ds)
        return t32[dx, 2 * dy + dz]

    got(rs_a, rs1.at[0], to_left)
    for i in range(2):
        for dz in range(NZH):
            q[0, i, dz] = (term(right, i, dz) + rs_a[i, dz].astype(F32)).astype(BF16)
    go(q.at[0], rs_e, rs1.at[4], to_right)
    got(rs_c, rs1.at[2], to_right)
    for i in range(2):
        for dz in range(NZH):
            q[1, i, dz] = (term(left, 2 + i, dz) + rs_c[i, dz].astype(F32)).astype(BF16)
    go(q.at[1], rs_f, rs1.at[5], to_left)

    opposite = m4(s + 2)
    for k in ORDER[:2]:
        got(piece(m4(f + k), opposite), agfl.at[k], dev_fs(f, s_left))
        pass_on(k, opposite)
    for k in ORDER[2:]:
        got(piece(m4(f + k), opposite), agfr.at[k], dev_fs(f, s_right))
        pass_on(k, opposite)

    got(rs_d, rs1.at[3], to_right)
    got(rs_e, rs1.at[4], to_left)
    got(rs_b, rs1.at[1], to_left)
    got(rs_f, rs1.at[5], to_right)
    for i in range(2):
        for dz in range(NZH):
            u[i, dz] = term(f, i, dz) + rs_d[i, dz].astype(F32) + rs_e[i, dz].astype(F32)
            u_send[i, dz] = u[i, dz].astype(BF16)
            u[2 + i, dz] = term(f, 2 + i, dz) + rs_b[i, dz].astype(F32) + rs_f[i, dz].astype(F32)
            u_send[2 + i, dz] = u[2 + i, dz].astype(BF16)
    for k in (1, 3, 2):
        go(u_send.at[m4(s + k)], u_recv.at[4 - k], rs2.at[4 - k], dev_fs(f, m4(s + k)))

    far = pl.ds(4 - half, 4)
    got(w.at[:, far], agp, partner)
    weight_all = w[...].reshape(model, key)
    lg[...] = jnp.zeros_like(lg)
    rows2 = 64

    @pl.loop(0, tokens // rows2)
    def _(i):
        block = pl.ds(pl.multiple_of(i * rows2, rows2), rows2)
        grad = lax.dot_general(
            grads[block, :], w[...].reshape(model, key), (((1,), (1,)), ((), ())),
            preferred_element_type=F32,
        )
        r = inv[block, :][:, :1]
        normed = act[block, :].astype(F32) * r
        both = grad * normed
        lg[...] += jnp.sum(both.reshape(rows2 // 8, 8, model), axis=0)
        mean = jnp.sum(both * gain[...], axis=1, keepdims=True) * (1.0 / model)
        out[block, :] = (r * (gain[...] * grad - normed * mean)).astype(BF16)

    line = jnp.sum(lg[...], axis=0, keepdims=True)
    for j in range(model // 128):
        g_own[j : j + 1, :] = line[:, 128 * j : 128 * (j + 1)]
    go(g_own, g_part, gp, partner)
    got(g_part, gp, partner)
    g_x[x] = g_own[...] + g_part[...]
    for k in range(1, NX):
        go(g_x.at[x], g_x.at[x], gx.at[4 - k], dev(m4(x + k), y, z, core))

    for k in range(1, 4):
        got(u_recv.at[k], rs2.at[k], dev_fs(f, m4(s + k)))
    for dz in range(NZH):
        v[dz] = (
            (u[s, dz] + u_recv[1, dz].astype(F32))
            + (u_recv[2, dz].astype(F32) + u_recv[3, dz].astype(F32))
        )

    for k in range(1, NX):
        got(g_x.at[m4(x + k)], gx.at[k], dev(m4(x + k), y, z, core))
    g_y[y] = (g_x[0] + g_x[1]) + (g_x[2] + g_x[3])
    for k in range(1, NY):
        go(g_y.at[y], g_y.at[y], gy.at[4 - k], dev(x, m4(y + k), z, core))

    lane = lax.broadcasted_iota(jnp.int32, (24, 128), 1)
    for dz in range(NZH):
        for pair in range(NZL // 2):
            top = v[dz, 0:24, 128 * pair : 128 * (pair + 1)]
            low = v[dz, 24:48, 128 * pair : 128 * (pair + 1)]
            z_send[dz * NZL + 2 * pair, 0:24] = jnp.where(lane < 64, top, pltpu.roll(low, 64, 1))
            z_send[dz * NZL + 2 * pair + 1, 0:24] = jnp.where(lane < 64, pltpu.roll(top, 64, 1), low)
    for k in range(1, NY):
        got(g_y.at[m4(y + k)], gy.at[k], dev(x, m4(y + k), z, core))
    g_own_xy = [(g_y[0, pl.ds(4 * x + pair, 1)] + g_y[1, pl.ds(4 * x + pair, 1)])
                + (g_y[2, pl.ds(4 * x + pair, 1)] + g_y[3, pl.ds(4 * x + pair, 1)]) for pair in range(NZL // 2)]
    for dz in range(NZ):
        z_send[dz, 24:32] = jnp.broadcast_to(g_own_xy[(dz % NZL) // 2], (8, 128))
    for k in range(1, NZ):
        there = lax.rem(z + k, NZ)
        go(z_send.at[there], z_recv.at[z], zsem.at[NZ - k], dev(x, y, there, core))
    z_recv[z] = z_send[z]
    for k in range(1, NZ):
        there = lax.rem(z + k, NZ)
        got(z_recv.at[there], zsem.at[k], dev(x, y, there, core))
    total = z_recv[0]
    for k in range(1, NZ):
        total = total + z_recv[k]
    total = total * (1.0 / 16)
    tail[0:24] = total[0:24]
    tail[24:32] = jnp.where(lax.rem(zl, 2) == 1, pltpu.roll(total[24:32], 64, 1), total[24:32])

    @pl.when(mine)
    def _():
        for n, off in enumerate(z_offsets):
            z_copy(n, off).wait_send()

    for made in sent:
        if made is not None:
            made.wait_send()


def local(activations, norm_gain, key_weight, key_grads):
    tokens, model = activations.shape
    key = key_grads.shape[1]
    dma = pltpu.SemaphoreType.DMA
    half_chunk = pltpu.VMEM((2, NZH, 48, 512), BF16)
    scratch = [
        pltpu.VMEM((tokens, model), BF16),
        pltpu.VMEM((tokens, 128), F32),
        pltpu.VMEM((16, 48, tokens), BF16),
        pltpu.VMEM((NX, NZL, 4, 16, key), BF16),
        pltpu.VMEM((NX, 8, 48, 512), F32),
        pltpu.VMEM((NX, 8, 48, 512), BF16),
        pltpu.VMEM((NX, 8, 48, 512), BF16),
        pltpu.VMEM((4, 4, NZH, 48, 512), BF16),
        half_chunk, half_chunk, half_chunk, half_chunk, half_chunk, half_chunk,
        pltpu.VMEM((2, 2, NZH, 48, 512), BF16),
        pltpu.VMEM((4, NZH, 48, 512), F32),
        pltpu.VMEM((4, NZH, 48, 512), BF16),
        pltpu.VMEM((4, NZH, 48, 512), BF16),
        pltpu.VMEM((NZH, 48, 512), F32),
        pltpu.VMEM((NZ, 32, 128), F32),
        pltpu.VMEM((NZ, 32, 128), F32),
        pltpu.VMEM((8, model), F32),
        pltpu.VMEM((16, 128), F32),
        pltpu.VMEM((16, 128), F32),
        pltpu.VMEM((NX, 16, 128), F32),
        pltpu.VMEM((NY, 16, 128), F32),
        dma((96,)),
        dma((4,)),
        dma((4,)), dma((4,)), dma((4,)), dma((4,)), dma((4,)),
        dma,
        dma((NX,)),
        dma((6,)),
        dma((4,)),
        dma((NZ,)),
        dma,
        dma((4,)),
        dma((4,)),
    ]
    vmem = pl.BlockSpec(memory_space=pltpu.VMEM)
    input_grads, tail = pl.pallas_call(
        kernel,
        out_shape=(
            jax.ShapeDtypeStruct((tokens, model), BF16),
            jax.ShapeDtypeStruct((32, 128), F32),
        ),
        in_specs=[vmem] * 4,
        out_specs=(vmem, vmem),
        scratch_shapes=scratch,
        compiler_params=pltpu.CompilerParams(
            collective_id=0, has_side_effects=True, vmem_limit_bytes=60 * 1024 * 1024
        ),
    )(activations, norm_gain.reshape(1, model), key_weight.reshape(4, 16, key), key_grads)
    packed = tail[:24]
    weight_grads = jnp.concatenate([packed[:, :64], packed[:, 64:]], axis=0).T
    return input_grads, weight_grads, tail[24, :64]


def solution(mesh):
    return jax.shard_map(
        local,
        mesh=mesh,
        in_specs=(P(("grp", "sub"), None), P(), P("sub", None), P(("grp", "sub"), None)),
        out_specs=(P(("grp", "sub"), None), P("sub", "grp"), P("sub")),
        check_vma=False,
    )
```

time: 570 us -> 84.2 us (0.15)
  waiting for transfers between devices: 393 us -> 0 us
  blocking collectives: 120 us -> 0 us
  Pallas kernels: 0 us -> 77.5 us
  starting transfers between devices: 16.2 us -> 0 us
  between operations: 15.5 us -> 0.64 us
  matrix products: 12.1 us -> 0 us
  other arithmetic: 10.4 us -> 0.61 us
    all_gather x1 -> x0, waiting for transfers between devices: 392 us -> none  [local(): lax.all_gather(key_weight, 'sub', axis=0, tiled=True)]
    psum x1 -> x0, blocking collectives: 120 us -> none  [local(): summed = lax.psum(local_gain, ('grp', 'sub'))]
    pallas_call x0 -> x1, Pallas kernels: none -> 77.5 us  [local(): pl.pallas_call(kernel, out_shape=(jax.ShapeDtypeStruct((tokens, model), B...]
    all_to_all x1 -> x0, starting transfers between devices: 16.2 us -> none  [local(): lax.all_to_all(term, 'sub', split_axis=0, concat_axis=1, tiled=True)]
    dot_general x2 -> x0, matrix products: 12.1 us -> none  [the longest x1 6.2 us: local(): lax.dot_general(scaled, key_grads, (((0,), (0,)), ((), ())), preferred_el...]
  transfers between devices with their start and end apart: 3 -> 0, of which waited for: 1 -> 0; matrix products, arithmetic and copies ran while one was open for 2% -> 0% of each run, Pallas kernels for 0% -> 0%
where the time goes in v1:
time: 84.2 us; the launch traced here: 83.9 us
  Pallas kernels  77.5 us (92%)
  local copies, waits for them, and re-layouts  5.2 us (6%)
    pallas_call x1, Pallas kernels, local(): pl.pallas_call(kernel, out_shape=(jax.ShapeDtypeStruct((tokens, model), B...  77.5 us
    unnamed x1, local copies, waits for them, and re-layouts  3.16 us

profile of v1, /device:TPU:1, one launch (start us, length us, event | category | flops | bytes accessed | tf_op | source)
XLA Modules:
  0.0 83.9 jit_solution(15339427939790198755)
XLA Ops:
  0.6 77.5 %shard_map.67 = (bf16[512,2048]{1,0:T(8,128)(2,1)}, f32[32,128]{1,0:T(8,128)}) custom-call(bf16[512,2048]{1,0:T(8,128)(2,1)} %act.1, f32[1,2048]{1,0:T(1,128)} %bitcast.7, bf16[4,16,768]{2,1,0:T(8,128)(2,1)} %bitcast.6, bf16[512,768]{1,0:T(8,128)(2,1)} %grads.1), custom_call_target="tpu_custom_call" | custom-call | tf_op jit(solution)/shard_map/pallas_call | solution.py:357
  78.1 1.2 %slice_bitcast_fusion = f32[64]{0:T(128)} fusion(f32[32,128]{1,0:T(8,128)} %get-tuple-element.6), kind=kLoop, calls=%fused_computation.1 | loop fusion | bytes 512 | tf_op jit(solution)/shard_map/squeeze | solution.py:372
  79.3 0.9 %fusion = (f32[24,64]{1,0:T(8,128)S(1)}, f32[24,64]{1,0:T(8,128)S(1)}) fusion(f32[32,128]{1,0:T(8,128)} %get-tuple-element.6), kind=kLoop, calls=%fused_computation.2 | loop fusion | bytes 24576 | tf_op jit(solution)/shard_map/slice | solution.py:371
  80.1 0.6 maximum_bitcast_fusion
  80.7 3.2 %copy.8 = bf16[512,2048]{1,0:T(8,128)(2,1)} copy(bf16[512,2048]{1,0:T(8,128)(2,1)} %get-tuple-element.12) | data formatting | bytes 4194304

commit v2 on v0

v2 whole, which is shorter than its diff:
```python
import functools

import jax
import jax.numpy as jnp
from jax import lax
from jax.experimental import pallas as pl
from jax.experimental.pallas import tpu as pltpu
from jax.sharding import PartitionSpec as P

MESH = pl.DeviceIdType.MESH
F32 = jnp.float32
BF16 = jnp.bfloat16
NX, NY, NZL, NZH = 4, 4, 8, 2
NZ = NZL * NZH
Z_ORDER = (8, 7, 9, 6, 10, 5, 11, 4, 12, 3, 13, 2, 14, 1, 15)
S_Z, S_P, S_W, S_PASS, S_ZP, S_RS1, S_RS2, S_ZT, S_GX, S_GY, S_GZ = range(11)


def kernel(
    act_hbm, gain_hbm, weight, grads_hbm,
    out, tail,
    act, gain, grads, gs, row_sum, scaled, inv, grads_t, w, t_give, t_keep, p_send, p_recv, give, given, p, r1, u, u_recv,
    v, z_send, z_recv, lg, g_x, g_y, gz_send, gz_recv,
    load, send, agz, ag1, ag2l, ag2r, agfl, agfr, agp, rsp, rsz, rs1, rs2, zsem, gx, gy, gz,
):
    g_idx, s_idx = lax.axis_index("grp"), lax.axis_index("sub")
    core = lax.rem(g_idx, 2)
    zh = lax.rem(lax.div(g_idx, 2), 2)
    y = lax.div(g_idx, 4)
    x = lax.div(s_idx, NZL)
    zl = lax.rem(s_idx, NZL)
    z = zh * NZL + zl
    f = x + core * (y - x)
    s = y + core * (x - y)
    tokens, model = act.shape
    key = grads.shape[1]

    def dev(dx, dy, dz, dc):
        return ((dy * 2 + lax.div(dz, NZL)) * 2 + dc, dx * NZL + lax.rem(dz, NZL))

    def xy(df, ds):
        return df + core * (ds - df), ds + core * (df - ds)

    def dev_fs(df, ds):
        dx, dy = xy(df, ds)
        return dev(dx, dy, z, core)

    def m4(a):
        return lax.rem(a, 4)

    partner = dev(x, y, z, 1 - core)
    right, left = m4(f + 1), m4(f + 3)
    s_right, s_left = m4(s + 1), m4(s + 3)

    def go(src, dst, group, recv, device):
        pltpu.make_async_remote_copy(
            src_ref=src, dst_ref=dst, send_sem=send.at[group], recv_sem=recv,
            device_id=device, device_id_type=MESH,
        ).start()

    def left_here(ref, group):
        pltpu.make_async_remote_copy(
            src_ref=ref, dst_ref=ref, send_sem=send.at[group], recv_sem=send.at[group],
            device_id=partner, device_id_type=MESH,
        ).wait_send()

    def got(dst, recv, device):
        pltpu.make_async_remote_copy(
            src_ref=dst, dst_ref=dst, send_sem=send.at[0], recv_sem=recv,
            device_id=device, device_id_type=MESH,
        ).wait_recv()

    barrier = pltpu.get_barrier_semaphore()
    peers = [partner]
    peers += [dev(m4(x + k), y, z, core) for k in range(1, NX)]
    peers += [dev(m4(x + k), y, z, 1 - core) for k in range(1, NX)]
    peers += [dev(x, m4(y + k), z, core) for k in range(1, NY)]
    peers += [dev(x, y, lax.rem(z + k, NZ), core) for k in range(1, NZ)]
    for peer in peers:
        pl.semaphore_signal(barrier, inc=1, device_id=peer, device_id_type=MESH)

    quarter = tokens // 4
    loads = [
        pltpu.make_async_copy(
            act_hbm.at[pl.ds(i * quarter, quarter)], act.at[pl.ds(i * quarter, quarter)], load.at[i]
        )
        for i in range(4)
    ]
    loads.append(pltpu.make_async_copy(gain_hbm, gain, load.at[4]))
    loads.append(pltpu.make_async_copy(grads_hbm, grads, load.at[5]))
    for i in (4, 0, 1, 2, 3, 5):
        loads[i].start()

    pl.semaphore_wait(barrier, len(peers))

    half = 4 * core
    mine = lax.div(zl, 4) == core
    z_offsets = (4, 3, 13, 2, 14, 1, 15)

    own_rows = pltpu.make_async_copy(weight.at[y], w.at[x, zl, y], load.at[6])

    @pl.when(mine)
    def _():
        for off in z_offsets:
            to = dev(x, y, lax.rem(z + off, NZ), core)
            go(weight.at[y], w.at[x, zl, y], S_Z, agz.at[lax.rem(zl, 4)], to)
        own_rows.start()

    rows = 64
    loads[4].wait()

    @pl.loop(0, tokens // rows)
    def _(i):
        @pl.when(lax.rem(i, 2) == 0)
        def _():
            at = pl.ds(pl.multiple_of(lax.div(i, 2) * quarter, quarter), quarter)
            pltpu.make_async_copy(act_hbm.at[at], act.at[at], load.at[lax.div(i, 2)]).wait()

        block = pl.ds(pl.multiple_of(i * rows, rows), rows)
        a = act[block, :].astype(F32)
        r = lax.rsqrt(jnp.sum(a * a, axis=1, keepdims=True) * (1.0 / model) + 1e-05)
        inv[block, :] = jnp.broadcast_to(r, (rows, 128))
        scaled[block, :] = (a * r * gain[...]).astype(BF16)

    loads[5].wait()
    grads_t[...] = grads[...].T.reshape(16, 48, tokens)

    keep_half = lax.rem(z, 2)
    half_keep = 4 * keep_half
    to_self = lax.div(zl, 4) == keep_half
    up, down = dev(x, y, lax.rem(z + 1, NZ), core), dev(x, y, lax.rem(z + NZ - 1, NZ), core)

    def product(parity, i, side):
        lhs = jnp.concatenate([grads_t[2 * j + parity] for j in range(8)], axis=0)
        rhs = scaled[:, pl.ds(pl.multiple_of(i * 512 + side * 256, 256), 256)]
        return jnp.dot(lhs, rhs, preferred_element_type=F32).reshape(8, 48, 256)

    def for_partner(n, side):
        @pl.loop(0, NX)
        def _(i):
            p_send[n, i] = product(1 - core, i, side).astype(BF16)
            go(p_send.at[n, i], p_recv.at[n, i], S_P, rsp.at[NX * n + i], partner)

    for_partner(0, 1 - keep_half)

    @pl.loop(0, NX)
    def _(i):
        t_give[i] = product(core, i, 1 - keep_half)

    @pl.loop(0, NX)
    def _(i):
        got(p_recv.at[0, i], rsp.at[i], partner)
        for j in range(8):
            give[i, j] = (t_give[i, j] + p_recv[0, i, j].astype(F32)).astype(BF16)
        go(give.at[i, pl.ds(0, 4)], given.at[i, pl.ds(0, 4)], S_ZP, rsz.at[i], up)
        go(give.at[i, pl.ds(4, 4)], given.at[i, pl.ds(4, 4)], S_ZP, rsz.at[NX + i], down)

    for_partner(1, keep_half)

    @pl.loop(0, NX)
    def _(i):
        t_keep[i] = product(core, i, keep_half)


    def piece(df, ds):
        dx, dy = xy(df, ds)
        return w.at[dx, pl.ds(half, 4), dy]

    def pass_on(k, ds):
        at = piece(m4(f + k), ds)
        go(at, at, S_PASS, agp.at[xy(m4(f + k), ds)[0]], partner)

    to_right, to_left = dev_fs(right, s), dev_fs(left, s)
    to_s_right, to_s_left = dev_fs(f, s_right), dev_fs(f, s_left)
    opposite = m4(s + 2)

    def spread(k):
        at = piece(m4(f + k), s)
        go(at, at, S_W, ag2l.at[k], to_s_right)
        go(at, at, S_W, ag2r.at[k], to_s_left)

    for i in range(4):
        @pl.when(half + i != zl)
        def _():
            got(w.at[x, half + i, y], agz.at[i], partner)

    @pl.when(mine)
    def _():
        own_rows.wait()

    own = piece(f, s)
    for k in (1, 3, 2):
        go(own, own, S_W, ag1.at[4 - k], dev_fs(m4(f + k), s))
    spread(0)
    pass_on(0, s)

    @pl.loop(0, NX)
    def _(i):
        got(p_recv.at[1, i], rsp.at[NX + i], partner)
        for j in range(8):
            t_keep[i, j] += p_recv[1, i, j].astype(F32)

    def first_axis(k):
        got(piece(m4(f + k), s), ag1.at[k], dev_fs(m4(f + k), s))
        spread(k)
        if k == 2:
            at = piece(m4(f + k), s)
            go(at, at, S_W, agfr.at[2], dev_fs(f, opposite))
        pass_on(k, s)

    def second_axis(k):
        at = piece(m4(f + k), s_left)
        got(at, ag2l.at[k], to_s_left)
        if k in (0, 1):
            go(at, at, S_W, agfl.at[k], to_s_right)
        pass_on(k, s_left)
        at = piece(m4(f + k), s_right)
        got(at, ag2r.at[k], to_s_right)
        if k == 3:
            go(at, at, S_W, agfr.at[k], to_s_left)
        pass_on(k, s_right)

    def across(k):
        sem, device = {
            0: (agfl, to_s_left), 1: (agfl, to_s_left), 3: (agfr, to_s_right), 2: (agfr, dev_fs(f, opposite)),
        }[k]
        got(piece(m4(f + k), opposite), sem.at[k], device)
        pass_on(k, opposite)

    first_axis(1)
    first_axis(3)
    second_axis(0)
    first_axis(2)

    @pl.loop(0, NX)
    def _(i):
        got(given.at[i, pl.ds(0, 4)], rsz.at[i], down)
        got(given.at[i, pl.ds(4, 4)], rsz.at[NX + i], up)
        for dy in range(NY):
            df, ds = xy(i, dy)
            for dz in range(NZH):
                total = t_keep[i, 2 * dy + dz] + given[i, 2 * dy + dz].astype(F32)
                t_keep[i, 2 * dy + dz] = total
                p[df, ds, dz] = total.astype(BF16)

    for k in (1, 3, 2):
        go(p.at[m4(f + k)], r1.at[3 - k], S_RS1, rs1, dev_fs(m4(f + k), s))

    second_axis(1)
    second_axis(3)
    across(0)

    far = pl.ds(4 - half, 4)
    rows2 = 256
    lg[...] = jnp.zeros_like(lg)
    row_sum[...] = jnp.zeros_like(row_sum)

    def features(dx):
        got(w.at[dx, far], agp.at[dx], partner)
        columns = pl.ds(pl.multiple_of(dx * 512, 512), 512)

        @pl.loop(0, tokens // rows2)
        def _(i):
            block = pl.ds(pl.multiple_of(i * rows2, rows2), rows2)
            grad = lax.dot_general(
                grads[block, :], w[dx].reshape(512, key), (((1,), (1,)), ((), ())),
                preferred_element_type=F32,
            )
            gs[block, columns] = grad
            both = grad * (act[block, columns].astype(F32) * inv[block, :][:, :1])
            lg[:, columns] += jnp.sum(both.reshape(rows2 // 8, 8, 512), axis=0)
            both = both * gain[:, columns]
            row_sum[block, :] += (both[:, 0:128] + both[:, 128:256]) + (both[:, 256:384] + both[:, 384:512])

    features(x)

    second_axis(2)
    across(1)
    across(3)
    across(2)

    features(m4(x + 1))

    features(m4(x + 3))
    features(m4(x + 2))

    line = jnp.sum(lg[...], axis=0, keepdims=True)
    own_x = 2 * x + core
    for j in range(model // 128):
        g_x[own_x, j : j + 1, :] = line[:, 128 * j : 128 * (j + 1)]
    x_peers = [(k, dc) for k in range(NX) for dc in range(2) if k or dc]

    def x_dev(k, dc):
        return dev(m4(x + k), y, z, core + dc * (1 - 2 * core))

    for k, dc in x_peers:
        go(g_x.at[own_x], g_x.at[own_x], S_GX, gx, x_dev(k, dc))

    got(r1, rs1, to_right)
    for i in range(NY):
        dx, dy = xy(f, i)
        for dz in range(NZH):
            u[i, dz] = (t_keep[dx, 2 * dy + dz] + r1[0, i, dz].astype(F32)) + (
                r1[1, i, dz].astype(F32) + r1[2, i, dz].astype(F32)
            )
    for k in (1, 3, 2):
        go(u.at[m4(s + k)], u_recv.at[3 - k], S_RS2, rs2, dev_fs(f, m4(s + k)))

    got(g_x.at[pl.ds(0, 7)], gx, partner)
    g_y[y] = ((g_x[0] + g_x[1]) + (g_x[2] + g_x[3])) + ((g_x[4] + g_x[5]) + (g_x[6] + g_x[7]))
    for k in range(1, NY):
        go(g_y.at[y], g_y.at[y], S_GY, gy, dev(x, m4(y + k), z, core))

    got(u_recv, rs2, to_s_left)
    for dz in range(NZH):
        v[dz] = (u[s, dz] + u_recv[0, dz]) + (u_recv[1, dz] + u_recv[2, dz])

    lane = lax.broadcasted_iota(jnp.int32, (24, 128), 1)
    z_there = []
    for dz in range(NZH):
        for pair in range(2):
            top = v[dz, 0:24, 128 * pair : 128 * (pair + 1)]
            low = v[dz, 24:48, 128 * pair : 128 * (pair + 1)]
            z_send[4 * dz + 2 * pair] = jnp.where(lane < 64, top, pltpu.roll(low, 64, 1))
            z_send[4 * dz + 2 * pair + 1] = jnp.where(lane < 64, pltpu.roll(top, 64, 1), low)
            z_there += [NZL * dz + half_keep + 2 * pair, NZL * dz + half_keep + 2 * pair + 1]
    z_slot = lax.div(z, 2)
    for i in (7, 0, 6, 1, 5, 2, 4, 3):
        @pl.when(z_there[i] != z)
        def _():
            go(z_send.at[i], z_recv.at[z_slot], S_ZT, zsem, dev(x, y, z_there[i], core))

        @pl.when(z_there[i] == z)
        def _():
            z_recv[z_slot] = z_send[i]

    def inputs(i):
        @pl.loop(0, quarter // 64)
        def _(j):
            block = pl.ds(pl.multiple_of(i * quarter + j * 64, 64), 64)
            r = inv[block, :][:, :1]
            mean = jnp.sum(row_sum[block, :], axis=1, keepdims=True) * (1.0 / model)
            normed = act[block, :].astype(F32) * r
            out[block, :] = (r * (gain[...] * gs[block, :] - normed * mean)).astype(BF16)

    inputs(0)
    inputs(1)

    got(g_y.at[pl.ds(0, 3)], gy, partner)
    for pair in range(NZL // 2):
        row = pl.ds(4 * x + pair, 1)
        value = (g_y[0, row] + g_y[1, row]) + (g_y[2, row] + g_y[3, row])
        for dz in range(NZH):
            gz_send[dz * NZL + 2 * pair] = value
            gz_send[dz * NZL + 2 * pair + 1] = value
    for k in Z_ORDER:
        there = lax.rem(z + k, NZ)
        go(gz_send.at[there], gz_recv.at[z], S_GZ, gz, dev(x, y, there, core))
    gz_recv[z] = gz_send[z]

    inputs(2)
    inputs(3)

    @pl.when(to_self)
    def _():
        got(z_recv.at[pl.ds(0, 7)], zsem, partner)

    @pl.when(jnp.logical_not(to_self))
    def _():
        got(z_recv, zsem, partner)

    total = z_recv[0]
    for k in range(1, 8):
        total = total + z_recv[k]
    tail[0:24] = total * (1.0 / 16)

    got(gz_recv.at[pl.ds(0, NZ - 1)], gz, partner)
    total = gz_recv[0]
    for k in range(1, NZ):
        total = total + gz_recv[k]
    total = jnp.broadcast_to(total * (1.0 / 16), (8, 128))
    tail[24:32] = jnp.where(lax.rem(zl, 2) == 1, pltpu.roll(total, 64, 1), total)

    @pl.when(mine)
    def _():
        left_here(w.at[0, pl.ds(0, 7), 0], S_Z)

    left_here(p_send, S_P)
    left_here(w.at[pl.ds(0, 3), pl.ds(0, 5)], S_W)
    left_here(w.at[:, pl.ds(0, 4)], S_PASS)
    left_here(p.at[pl.ds(0, 3)], S_RS1)
    left_here(give, S_ZP)
    left_here(u.at[pl.ds(0, 3)], S_RS2)

    @pl.when(to_self)
    def _():
        left_here(z_send.at[pl.ds(0, 7)], S_ZT)

    @pl.when(jnp.logical_not(to_self))
    def _():
        left_here(z_send, S_ZT)

    left_here(g_x.at[pl.ds(0, 7)], S_GX)
    left_here(g_y.at[pl.ds(0, 3)], S_GY)
    left_here(gz_send.at[pl.ds(0, NZ - 1)], S_GZ)


def finish(raw, tail, out, weight_grads, gain_grads, buf, come, leave):
    away = pltpu.make_async_copy(raw, out, leave)
    away.start()
    into = pltpu.make_async_copy(tail, buf, come)
    into.start()
    into.wait()
    weight_grads[0:24] = buf[0:24, 0:64]
    weight_grads[24:48] = buf[0:24, 64:128]
    gain_grads[...] = buf[24:25, 0:64]
    away.wait()


def local(activations, norm_gain, key_weight, key_grads):
    tokens, model = activations.shape
    key = key_grads.shape[1]
    dma = pltpu.SemaphoreType.DMA
    scratch = [
        pltpu.VMEM((tokens, model), BF16),
        pltpu.VMEM((1, model), F32),
        pltpu.VMEM((tokens, key), BF16),
        pltpu.VMEM((tokens, model), F32),
        pltpu.VMEM((tokens, 128), F32),
        pltpu.VMEM((tokens, model), BF16),
        pltpu.VMEM((tokens, 128), F32),
        pltpu.VMEM((16, 48, tokens), BF16),
        pltpu.VMEM((NX, NZL, 4, 16, key), BF16),
        pltpu.VMEM((NX, 8, 48, 256), F32),
        pltpu.VMEM((NX, 8, 48, 256), F32),
        pltpu.VMEM((2, NX, 8, 48, 256), BF16),
        pltpu.VMEM((2, NX, 8, 48, 256), BF16),
        pltpu.VMEM((NX, 8, 48, 256), BF16),
        pltpu.VMEM((NX, 8, 48, 256), BF16),
        pltpu.VMEM((4, 4, NZH, 48, 256), BF16),
        pltpu.VMEM((3, 4, NZH, 48, 256), BF16),
        pltpu.VMEM((4, NZH, 48, 256), F32),
        pltpu.VMEM((3, NZH, 48, 256), F32),
        pltpu.VMEM((NZH, 48, 256), F32),
        pltpu.VMEM((8, 24, 128), F32),
        pltpu.VMEM((8, 24, 128), F32),
        pltpu.VMEM((8, model), F32),
        pltpu.VMEM((2 * NX, 16, 128), F32),
        pltpu.VMEM((NY, 16, 128), F32),
        pltpu.VMEM((NZ, 1, 128), F32),
        pltpu.VMEM((NZ, 1, 128), F32),
        dma((7,)),
        dma((11,)),
        dma((4,)),
        dma((4,)), dma((4,)), dma((4,)), dma((4,)), dma((4,)),
        dma((NX,)),
        dma((2 * NX,)),
        dma((2 * NX,)),
        dma,
        dma,
        dma,
        dma,
        dma,
        dma,
    ]
    vmem = pl.BlockSpec(memory_space=pltpu.VMEM)
    hbm = pl.BlockSpec(memory_space=pl.ANY)
    raw, tail = pl.pallas_call(
        kernel,
        out_shape=(
            pltpu.VMEM((tokens, model), BF16),
            pltpu.VMEM((32, 128), F32),
        ),
        in_specs=[hbm] * 4,
        out_specs=(vmem, vmem),
        scratch_shapes=scratch,
        compiler_params=pltpu.CompilerParams(
            collective_id=0, has_side_effects=True, vmem_limit_bytes=64900000
        ),
    )(activations, norm_gain.reshape(1, model), key_weight.reshape(4, 16, key), key_grads)
    input_grads, weight_grads, gain_grads = pl.pallas_call(
        finish,
        out_shape=(
            jax.ShapeDtypeStruct((tokens, model), BF16),
            jax.ShapeDtypeStruct((48, 64), F32),
            jax.ShapeDtypeStruct((1, 64), F32),
        ),
        in_specs=[hbm, hbm],
        out_specs=(hbm, vmem, vmem),
        scratch_shapes=[pltpu.VMEM((32, 128), F32), dma, dma],
        compiler_params=pltpu.CompilerParams(vmem_limit_bytes=1024 * 1024),
    )(raw, tail)
    return input_grads, weight_grads.T, gain_grads[0]


def solution(mesh):
    return jax.shard_map(
        local,
        mesh=mesh,
        in_specs=(P(("grp", "sub"), None), P(), P("sub", None), P(("grp", "sub"), None)),
        out_specs=(P(("grp", "sub"), None), P("sub", "grp"), P("sub")),
        check_vma=False,
    )
```

time: 570 us -> 62 us (0.11)
  waiting for transfers between devices: 393 us -> 0 us
  blocking collectives: 120 us -> 0 us
  Pallas kernels: 0 us -> 61.2 us
  starting transfers between devices: 16.2 us -> 0 us
  between operations: 15.5 us -> 0.64 us
  matrix products: 12.1 us -> 0 us
  other arithmetic: 10.4 us -> 0 us
    all_gather x1 -> x0, waiting for transfers between devices: 392 us -> none  [local(): lax.all_gather(key_weight, 'sub', axis=0, tiled=True)]
    psum x1 -> x0, blocking collectives: 120 us -> none  [local(): summed = lax.psum(local_gain, ('grp', 'sub'))]
    pallas_call x0 -> x2, Pallas kernels: none -> 61.2 us  [the longest x1 59.3 us: local(): pl.pallas_call(kernel, out_shape=(pltpu.VMEM((tokens, model), BF16), pltp...]
    all_to_all x1 -> x0, starting transfers between devices: 16.2 us -> none  [local(): lax.all_to_all(term, 'sub', split_axis=0, concat_axis=1, tiled=True)]
    dot_general x2 -> x0, matrix products: 12.1 us -> none  [the longest x1 6.2 us: local(): lax.dot_general(scaled, key_grads, (((0,), (0,)), ((), ())), preferred_el...]
  transfers between devices with their start and end apart: 3 -> 0, of which waited for: 1 -> 0; matrix products, arithmetic and copies ran while one was open for 2% -> 0% of each run, Pallas kernels for 0% -> 0%
where the time goes in v2:
time: 62 us; the launch traced here: 61.9 us
  Pallas kernels  61.2 us (99%)
  between operations  0.64 us (1%)
    pallas_call x1, Pallas kernels, local(): pl.pallas_call(kernel, out_shape=(pltpu.VMEM((tokens, model), BF16), pltp...  59.3 us
    pallas_call x1, Pallas kernels, local(): pl.pallas_call(finish, out_shape=(jax.ShapeDtypeStruct((tokens, model), B...  1.95 us

profile of v2, /device:TPU:1, one launch (start us, length us, event | category | flops | bytes accessed | tf_op | source)
XLA Modules:
  0.0 61.9 jit_solution(13978853774062537611)
XLA Ops:
  0.6 59.3 %shard_map.67 = (bf16[512,2048]{1,0:T(8,128)(2,1)S(1)}, f32[32,128]{1,0:T(8,128)S(1)}) custom-call(bf16[512,2048]{1,0:T(8,128)(2,1)} %act_hbm.1, f32[1,2048]{1,0:T(1,128)} %bitcast.5, bf16[4,16,768]{2,1,0:T(8,128)(2,1)} %bitcast.4, bf16[512,768]{1,0:T(8,128)(2,1)} %grads_hbm.1), custom_call_target="tpu_custom_call" | custom-call | tf_op jit(solution)/shard_map/pallas_call | solution.py:468
  59.9 1.9 %shard_map.68 = (bf16[512,2048]{1,0:T(8,128)(2,1)}, f32[48,64]{1,0:T(8,128)}, f32[1,64]{1,0:T(1,128)}) custom-call(bf16[512,2048]{1,0:T(8,128)(2,1)S(1)} %get-tuple-element.8.raw, f32[32,128]{1,0:T(8,128)S(1)} %get-tuple-element.9.tail), custom_call_target="tpu_custom_call" | custom-call | tf_op jit(solution)/shard_map/pallas_call | solution.py:481

commit v3 on v2

--- a/solution.py
+++ b/solution.py
@@ -13,15 +13,15 @@
 NX, NY, NZL, NZH = 4, 4, 8, 2
 NZ = NZL * NZH
 Z_ORDER = (8, 7, 9, 6, 10, 5, 11, 4, 12, 3, 13, 2, 14, 1, 15)
-S_Z, S_P, S_W, S_PASS, S_ZP, S_RS1, S_RS2, S_ZT, S_GX, S_GY, S_GZ = range(11)
+S_Z, S_P, S_W, S_PASS, S_ZP, S_RS1, S_RS2, S_ZT, S_GX, S_GZ = range(10)
 
 
 def kernel(
     act_hbm, gain_hbm, weight, grads_hbm,
     out, tail,
-    act, gain, grads, gs, row_sum, scaled, inv, grads_t, w, t_give, t_keep, p_send, p_recv, give, given, p, r1, u, u_recv,
-    v, z_send, z_recv, lg, g_x, g_y, gz_send, gz_recv,
-    load, send, agz, ag1, ag2l, ag2r, agfl, agfr, agp, rsp, rsz, rs1, rs2, zsem, gx, gy, gz,
+    act, gain, grads, gs, row_sum, scaled, inv, grads_t, w, both, t_give, t_keep, p_send, p_recv, give, given, p, r1, u, u_recv,
+    v, z_send, z_recv, lg, g_send, g_recv, gz_send, gz_recv,
+    load, send, agz, ag1, ag2l, ag2r, agf, agp, rsp, rsz, rs1, rs2, zsem, gx, gz, far_sem,
 ):
     g_idx, s_idx = lax.axis_index("grp"), lax.axis_index("sub")
     core = lax.rem(g_idx, 2)
@@ -72,10 +72,14 @@
 
     barrier = pltpu.get_barrier_semaphore()
     peers = [partner]
-    peers += [dev(m4(x + k), y, z, core) for k in range(1, NX)]
-    peers += [dev(m4(x + k), y, z, 1 - core) for k in range(1, NX)]
-    peers += [dev(x, m4(y + k), z, core) for k in range(1, NY)]
-    peers += [dev(x, y, lax.rem(z + k, NZ), core) for k in range(1, NZ)]
+    plane = [(dx, dy, dc) for dx in range(NX) for dy in (2, 1, 3, 0) for dc in range(2)]
+    plane.remove((0, 0, 0))
+
+    def plane_dev(dx, dy, dc):
+        return dev(m4(x + dx), m4(y + dy), z, core + dc * (1 - 2 * core))
+
+    peers += [plane_dev(*away) for away in plane if away != (0, 0, 1)]
+    peers += [dev(x, y, lax.rem(z + k, NZ), core) for k in (1, 2, 3, 4, 12, 13, 14, 15)]
     for peer in peers:
         pl.semaphore_signal(barrier, inc=1, device_id=peer, device_id_type=MESH)
 
@@ -91,21 +95,6 @@
     for i in (4, 0, 1, 2, 3, 5):
         loads[i].start()
 
-    pl.semaphore_wait(barrier, len(peers))
-
-    half = 4 * core
-    mine = lax.div(zl, 4) == core
-    z_offsets = (4, 3, 13, 2, 14, 1, 15)
-
-    own_rows = pltpu.make_async_copy(weight.at[y], w.at[x, zl, y], load.at[6])
-
-    @pl.when(mine)
-    def _():
-        for off in z_offsets:
-            to = dev(x, y, lax.rem(z + off, NZ), core)
-            go(weight.at[y], w.at[x, zl, y], S_Z, agz.at[lax.rem(zl, 4)], to)
-        own_rows.start()
-
     rows = 64
     loads[4].wait()
 
@@ -125,27 +114,44 @@
     loads[5].wait()
     grads_t[...] = grads[...].T.reshape(16, 48, tokens)
 
+    pl.semaphore_wait(barrier, len(peers))
+    for k in (4, 12):
+        pl.semaphore_signal(
+            far_sem, inc=1, device_id=dev(x, y, lax.rem(z + k, NZ), core), device_id_type=MESH
+        )
+
+    half = 4 * core
+    mine = lax.div(zl, 4) == core
+    z_offsets = (4, 3, 13, 2, 14, 1, 15)
+
+    own_rows = pltpu.make_async_copy(weight.at[y], w.at[x, zl, y], load.at[6])
+
+    @pl.when(mine)
+    def _():
+        for off in z_offsets:
+            to = dev(x, y, lax.rem(z + off, NZ), core)
+            go(weight.at[y], w.at[x, zl, y], S_Z, agz.at[lax.rem(zl, 4)], to)
+        own_rows.start()
+
     keep_half = lax.rem(z, 2)
     half_keep = 4 * keep_half
     to_self = lax.div(zl, 4) == keep_half
     up, down = dev(x, y, lax.rem(z + 1, NZ), core), dev(x, y, lax.rem(z + NZ - 1, NZ), core)
 
-    def product(parity, i, side):
-        lhs = jnp.concatenate([grads_t[2 * j + parity] for j in range(8)], axis=0)
+    def products(n, i, side, own):
         rhs = scaled[:, pl.ds(pl.multiple_of(i * 512 + side * 256, 256), 256)]
-        return jnp.dot(lhs, rhs, preferred_element_type=F32).reshape(8, 48, 256)
-
-    def for_partner(n, side):
-        @pl.loop(0, NX)
-        def _(i):
-            p_send[n, i] = product(1 - core, i, side).astype(BF16)
-            go(p_send.at[n, i], p_recv.at[n, i], S_P, rsp.at[NX * n + i], partner)
-
-    for_partner(0, 1 - keep_half)
+        both[...] = jnp.dot(
+            grads_t[...].reshape(key, tokens), rhs, preferred_element_type=F32
+        ).reshape(16, 48, 256)
+        for j in range(8):
+            p_send[n, i, j] = both[2 * j + 1 - core].astype(BF16)
+        go(p_send.at[n, i], p_recv.at[n, i], S_P, rsp.at[NX * n + i], partner)
+        for j in range(8):
+            own[i, j] = both[2 * j + core]
 
     @pl.loop(0, NX)
     def _(i):
-        t_give[i] = product(core, i, 1 - keep_half)
+        products(0, i, 1 - keep_half, t_give)
 
     @pl.loop(0, NX)
     def _(i):
@@ -155,11 +161,9 @@
         go(give.at[i, pl.ds(0, 4)], given.at[i, pl.ds(0, 4)], S_ZP, rsz.at[i], up)
         go(give.at[i, pl.ds(4, 4)], given.at[i, pl.ds(4, 4)], S_ZP, rsz.at[NX + i], down)
 
-    for_partner(1, keep_half)
-
     @pl.loop(0, NX)
     def _(i):
-        t_keep[i] = product(core, i, keep_half)
+        products(1, i, keep_half, t_keep)
 
 
     def piece(df, ds):
@@ -173,6 +177,7 @@
     to_right, to_left = dev_fs(right, s), dev_fs(left, s)
     to_s_right, to_s_left = dev_fs(f, s_right), dev_fs(f, s_left)
     opposite = m4(s + 2)
+    to_opposite = dev_fs(f, opposite)
 
     def spread(k):
         at = piece(m4(f + k), s)
@@ -189,7 +194,7 @@
         own_rows.wait()
 
     own = piece(f, s)
-    for k in (1, 3, 2):
+    for k in (2, 1, 3):
         go(own, own, S_W, ag1.at[4 - k], dev_fs(m4(f + k), s))
     spread(0)
     pass_on(0, s)
@@ -200,40 +205,7 @@
         for j in range(8):
             t_keep[i, j] += p_recv[1, i, j].astype(F32)
 
-    def first_axis(k):
-        got(piece(m4(f + k), s), ag1.at[k], dev_fs(m4(f + k), s))
-        spread(k)
-        if k == 2:
-            at = piece(m4(f + k), s)
-            go(at, at, S_W, agfr.at[2], dev_fs(f, opposite))
-        pass_on(k, s)
-
-    def second_axis(k):
-        at = piece(m4(f + k), s_left)
-        got(at, ag2l.at[k], to_s_left)
-        if k in (0, 1):
-            go(at, at, S_W, agfl.at[k], to_s_right)
-        pass_on(k, s_left)
-        at = piece(m4(f + k), s_right)
-        got(at, ag2r.at[k], to_s_right)
-        if k == 3:
-            go(at, at, S_W, agfr.at[k], to_s_left)
-        pass_on(k, s_right)
-
-    def across(k):
-        sem, device = {
-            0: (agfl, to_s_left), 1: (agfl, to_s_left), 3: (agfr, to_s_right), 2: (agfr, dev_fs(f, opposite)),
-        }[k]
-        got(piece(m4(f + k), opposite), sem.at[k], device)
-        pass_on(k, opposite)
-
-    first_axis(1)
-    first_axis(3)
-    second_axis(0)
-    first_axis(2)
-
-    @pl.loop(0, NX)
-    def _(i):
+    def chunk(i):
         got(given.at[i, pl.ds(0, 4)], rsz.at[i], down)
         got(given.at[i, pl.ds(4, 4)], rsz.at[NX + i], up)
         for dy in range(NY):
@@ -243,11 +215,45 @@
                 t_keep[i, 2 * dy + dz] = total
                 p[df, ds, dz] = total.astype(BF16)
 
-    for k in (1, 3, 2):
-        go(p.at[m4(f + k)], r1.at[3 - k], S_RS1, rs1, dev_fs(m4(f + k), s))
-
+            @pl.when(df != f)
+            def _():
+                go(p.at[df, ds], r1.at[3 - m4(df - f + 4), ds], S_RS1, rs1, dev_fs(df, s))
+
+    def first_axis(k):
+        got(piece(m4(f + k), s), ag1.at[k], dev_fs(m4(f + k), s))
+        spread(k)
+        if k == 2:
+            at = piece(m4(f + k), s)
+            go(at, at, S_W, agf.at[k], to_opposite)
+        pass_on(k, s)
+
+    def second_axis(k):
+        at = piece(m4(f + k), s_left)
+        got(at, ag2l.at[k], to_s_left)
+        if k in (0, 1):
+            go(at, at, S_W, agf.at[k], to_s_right)
+        pass_on(k, s_left)
+        at = piece(m4(f + k), s_right)
+        got(at, ag2r.at[k], to_s_right)
+        if k == 3:
+            go(at, at, S_W, agf.at[k], to_s_left)
+        pass_on(k, s_right)
+
+    def across(k):
+        got(piece(m4(f + k), opposite), agf.at[k], to_opposite)
+        pass_on(k, opposite)
+
+    chunk(0)
+    first_axis(1)
+    first_axis(3)
+    chunk(1)
+    second_axis(0)
+    first_axis(2)
     second_axis(1)
     second_axis(3)
+    chunk(2)
+    second_axis(2)
+    chunk(3)
     across(0)
 
     far = pl.ds(4 - half, 4)
@@ -267,34 +273,29 @@
                 preferred_element_type=F32,
             )
             gs[block, columns] = grad
-            both = grad * (act[block, columns].astype(F32) * inv[block, :][:, :1])
-            lg[:, columns] += jnp.sum(both.reshape(rows2 // 8, 8, 512), axis=0)
-            both = both * gain[:, columns]
-            row_sum[block, :] += (both[:, 0:128] + both[:, 128:256]) + (both[:, 256:384] + both[:, 384:512])
-
-    features(x)
-
-    second_axis(2)
+            prod = grad * (act[block, columns].astype(F32) * inv[block, :][:, :1])
+            lg[:, columns] += jnp.sum(prod.reshape(rows2 // 8, 8, 512), axis=0)
+            prod = prod * gain[:, columns]
+            row_sum[block, :] += (prod[:, 0:128] + prod[:, 128:256]) + (prod[:, 256:384] + prod[:, 384:512])
+
+    me = (x * NY + y) * 2 + core
+
+    def block(k):
+        there = m4(x + k)
+        features(there)
+        g_send[k] = jnp.sum(
+            lg[:, pl.ds(pl.multiple_of(there * 512, 512), 512)], axis=0, keepdims=True
+        )
+        for away in plane:
+            if away[0] == k:
+                go(g_send.at[k], g_recv.at[me], S_GX, gx, plane_dev(*away))
+
+    block(0)
+    g_recv[me] = g_send[0]
+
     across(1)
     across(3)
     across(2)
-
-    features(m4(x + 1))
-
-    features(m4(x + 3))
-    features(m4(x + 2))
-
-    line = jnp.sum(lg[...], axis=0, keepdims=True)
-    own_x = 2 * x + core
-    for j in range(model // 128):
-        g_x[own_x, j : j + 1, :] = line[:, 128 * j : 128 * (j + 1)]
-    x_peers = [(k, dc) for k in range(NX) for dc in range(2) if k or dc]
-
-    def x_dev(k, dc):
-        return dev(m4(x + k), y, z, core + dc * (1 - 2 * core))
-
-    for k, dc in x_peers:
-        go(g_x.at[own_x], g_x.at[own_x], S_GX, gx, x_dev(k, dc))
 
     got(r1, rs1, to_right)
     for i in range(NY):
@@ -306,10 +307,10 @@
     for k in (1, 3, 2):
         go(u.at[m4(s + k)], u_recv.at[3 - k], S_RS2, rs2, dev_fs(f, m4(s + k)))
 
-    got(g_x.at[pl.ds(0, 7)], gx, partner)
-    g_y[y] = ((g_x[0] + g_x[1]) + (g_x[2] + g_x[3])) + ((g_x[4] + g_x[5]) + (g_x[6] + g_x[7]))
-    for k in range(1, NY):
-        go(g_y.at[y], g_y.at[y], S_GY, gy, dev(x, m4(y + k), z, core))
+
+    block(2)
+    block(1)
+    block(3)
 
     got(u_recv, rs2, to_s_left)
     for dz in range(NZH):
@@ -325,6 +326,7 @@
             z_send[4 * dz + 2 * pair + 1] = jnp.where(lane < 64, pltpu.roll(top, 64, 1), low)
             z_there += [NZL * dz + half_keep + 2 * pair, NZL * dz + half_keep + 2 * pair + 1]
     z_slot = lax.div(z, 2)
+    pl.semaphore_wait(far_sem, 2)
     for i in (7, 0, 6, 1, 5, 2, 4, 3):
         @pl.when(z_there[i] != z)
         def _():
@@ -343,13 +345,12 @@
             normed = act[block, :].astype(F32) * r
             out[block, :] = (r * (gain[...] * gs[block, :] - normed * mean)).astype(BF16)
 
-    inputs(0)
-    inputs(1)
-
-    got(g_y.at[pl.ds(0, 3)], gy, partner)
+    got(g_recv.at[pl.ds(0, 31)], gx, partner)
+    line = g_recv[0]
+    for i in range(1, 32):
+        line = line + g_recv[i]
     for pair in range(NZL // 2):
-        row = pl.ds(4 * x + pair, 1)
-        value = (g_y[0, row] + g_y[1, row]) + (g_y[2, row] + g_y[3, row])
+        value = line[:, 128 * pair : 128 * (pair + 1)]
         for dz in range(NZH):
             gz_send[dz * NZL + 2 * pair] = value
             gz_send[dz * NZL + 2 * pair + 1] = value
@@ -358,6 +359,8 @@
         go(gz_send.at[there], gz_recv.at[z], S_GZ, gz, dev(x, y, there, core))
     gz_recv[z] = gz_send[z]
 
+    inputs(0)
+    inputs(1)
     inputs(2)
     inputs(3)
 
@@ -400,8 +403,7 @@
     def _():
         left_here(z_send, S_ZT)
 
-    left_here(g_x.at[pl.ds(0, 7)], S_GX)
-    left_here(g_y.at[pl.ds(0, 3)], S_GY)
+    left_here(g_recv.at[pl.ds(0, 31)], S_GX)
     left_here(gz_send.at[pl.ds(0, NZ - 1)], S_GZ)
 
 
@@ -431,6 +433,7 @@
         pltpu.VMEM((tokens, 128), F32),
         pltpu.VMEM((16, 48, tokens), BF16),
         pltpu.VMEM((NX, NZL, 4, 16, key), BF16),
+        pltpu.VMEM((16, 48, 256), F32),
         pltpu.VMEM((NX, 8, 48, 256), F32),
         pltpu.VMEM((NX, 8, 48, 256), F32),
         pltpu.VMEM((2, NX, 8, 48, 256), BF16),
@@ -445,14 +448,14 @@
         pltpu.VMEM((8, 24, 128), F32),
         pltpu.VMEM((8, 24, 128), F32),
         pltpu.VMEM((8, model), F32),
-        pltpu.VMEM((2 * NX, 16, 128), F32),
-        pltpu.VMEM((NY, 16, 128), F32),
+        pltpu.VMEM((NX, 1, 512), F32),
+        pltpu.VMEM((32, 1, 512), F32),
         pltpu.VMEM((NZ, 1, 128), F32),
         pltpu.VMEM((NZ, 1, 128), F32),
         dma((7,)),
-        dma((11,)),
+        dma((10,)),
         dma((4,)),
-        dma((4,)), dma((4,)), dma((4,)), dma((4,)), dma((4,)),
+        dma((4,)), dma((4,)), dma((4,)), dma((4,)),
         dma((NX,)),
         dma((2 * NX,)),
         dma((2 * NX,)),
@@ -461,7 +464,7 @@
         dma,
         dma,
         dma,
-        dma,
+        pltpu.SemaphoreType.REGULAR,
     ]
     vmem = pl.BlockSpec(memory_space=pltpu.VMEM)
     hbm = pl.BlockSpec(memory_space=pl.ANY)

time: 62 us -> 58 us (0.935)
  Pallas kernels: 61.2 us -> 57.2 us
    pallas_call x1, Pallas kernels: 59.3 us -> 55.3 us  [local(): pl.pallas_call(kernel, out_shape=(pltpu.VMEM((tokens, model), BF16), pltp...]
where the time goes in v3:
time: 58 us; the launch traced here: 57.9 us
  Pallas kernels  57.2 us (99%)
  between operations  0.64 us (1%)
    pallas_call x1, Pallas kernels, local(): pl.pallas_call(kernel, out_shape=(pltpu.VMEM((tokens, model), BF16), pltp...  55.3 us
    pallas_call x1, Pallas kernels, local(): pl.pallas_call(finish, out_shape=(jax.ShapeDtypeStruct((tokens, model), B...  1.95 us

profile of v3, /device:TPU:1, one launch (start us, length us, event | category | flops | bytes accessed | tf_op | source)
XLA Modules:
  0.0 57.9 jit_solution(1496137076794850809)
XLA Ops:
  0.6 55.3 %shard_map.67 = (bf16[512,2048]{1,0:T(8,128)(2,1)S(1)}, f32[32,128]{1,0:T(8,128)S(1)}) custom-call(bf16[512,2048]{1,0:T(8,128)(2,1)} %act_hbm.1, f32[1,2048]{1,0:T(1,128)} %bitcast.5, bf16[4,16,768]{2,1,0:T(8,128)(2,1)} %bitcast.4, bf16[512,768]{1,0:T(8,128)(2,1)} %grads_hbm.1), custom_call_target="tpu_custom_call" | custom-call | tf_op jit(solution)/shard_map/pallas_call | solution.py:471
  55.9 1.9 %shard_map.68 = (bf16[512,2048]{1,0:T(8,128)(2,1)}, f32[48,64]{1,0:T(8,128)}, f32[1,64]{1,0:T(1,128)}) custom-call(bf16[512,2048]{1,0:T(8,128)(2,1)S(1)} %get-tuple-element.8.raw, f32[32,128]{1,0:T(8,128)S(1)} %get-tuple-element.9.tail), custom_call_target="tpu_custom_call" | custom-call | tf_op jit(solution)/shard_map/pallas_call | solution.py:484

commit v4 on v3

--- a/solution.py
+++ b/solution.py
@@ -21,7 +21,7 @@
     out, tail,
     act, gain, grads, gs, row_sum, scaled, inv, grads_t, w, both, t_give, t_keep, p_send, p_recv, give, given, p, r1, u, u_recv,
     v, z_send, z_recv, lg, g_send, g_recv, gz_send, gz_recv,
-    load, send, agz, ag1, ag2l, ag2r, agf, agp, rsp, rsz, rs1, rs2, zsem, gx, gz, far_sem,
+    load, send, agz, ag1, ag2, agzz, agp, rsp, rsz, rs1, rs2, zsem, gx, gz, far_sem,
 ):
     g_idx, s_idx = lax.axis_index("grp"), lax.axis_index("sub")
     core = lax.rem(g_idx, 2)
@@ -49,8 +49,6 @@
         return lax.rem(a, 4)
 
     partner = dev(x, y, z, 1 - core)
-    right, left = m4(f + 1), m4(f + 3)
-    s_right, s_left = m4(s + 1), m4(s + 3)
 
     def go(src, dst, group, recv, device):
         pltpu.make_async_remote_copy(
@@ -166,23 +164,30 @@
         products(1, i, keep_half, t_keep)
 
 
-    def piece(df, ds):
-        dx, dy = xy(df, ds)
-        return w.at[dx, pl.ds(half, 4), dy]
-
-    def pass_on(k, ds):
-        at = piece(m4(f + k), ds)
-        go(at, at, S_PASS, agp.at[xy(m4(f + k), ds)[0]], partner)
-
-    to_right, to_left = dev_fs(right, s), dev_fs(left, s)
-    to_s_right, to_s_left = dev_fs(f, s_right), dev_fs(f, s_left)
-    opposite = m4(s + 2)
-    to_opposite = dev_fs(f, opposite)
-
-    def spread(k):
-        at = piece(m4(f + k), s)
-        go(at, at, S_W, ag2l.at[k], to_s_right)
-        go(at, at, S_W, ag2r.at[k], to_s_left)
+    side = (1 + 2 * keep_half, 3 - 2 * keep_half)
+
+    def piece(n, m, other=0):
+        k = (0, side[other], 2)[n]
+        dx, dy = xy(m4(f + k), m4(s + m))
+        if n < 2:
+            return w.at[dx, pl.ds(half, 4), dy], dx
+        return w.at[dx, pl.ds(half + 2 * (keep_half + other * (1 - 2 * keep_half)), 2), dy], dx
+
+    def pass_on(n, m, other=0):
+        at, dx = piece(n, m, other)
+        go(at, at, S_PASS, agp.at[dx], partner)
+
+    s_devs = [dev_fs(f, m4(s + m)) for m in range(4)]
+
+    def spread(n):
+        at, _ = piece(n, 0)
+        go(at, at, S_W, ag2.at[4 * n + 3], s_devs[1])
+        go(at, at, S_W, ag2.at[4 * n + 1], s_devs[3])
+
+    def along_z(n, m):
+        if n:
+            at, _ = piece(n, m)
+            go(at, at, S_W, agzz.at[4 * (n - 1) + m], up if n == 1 and m != 2 else down)
 
     for i in range(4):
         @pl.when(half + i != zl)
@@ -193,11 +198,13 @@
     def _():
         own_rows.wait()
 
-    own = piece(f, s)
-    for k in (2, 1, 3):
-        go(own, own, S_W, ag1.at[4 - k], dev_fs(m4(f + k), s))
+    dx, dy = xy(f, s)
+    own_half = w.at[dx, pl.ds(half + 2 * keep_half, 2), dy]
+    go(own_half, own_half, S_W, ag1.at[1], dev_fs(m4(f + 2), s))
+    own, _ = piece(0, 0)
+    go(own, own, S_W, ag1.at[0], dev_fs(m4(f + 3 + 2 * keep_half), s))
     spread(0)
-    pass_on(0, s)
+    pass_on(0, 0)
 
     @pl.loop(0, NX)
     def _(i):
@@ -219,42 +226,41 @@
             def _():
                 go(p.at[df, ds], r1.at[3 - m4(df - f + 4), ds], S_RS1, rs1, dev_fs(df, s))
 
-    def first_axis(k):
-        got(piece(m4(f + k), s), ag1.at[k], dev_fs(m4(f + k), s))
-        spread(k)
-        if k == 2:
-            at = piece(m4(f + k), s)
-            go(at, at, S_W, agf.at[k], to_opposite)
-        pass_on(k, s)
-
-    def second_axis(k):
-        at = piece(m4(f + k), s_left)
-        got(at, ag2l.at[k], to_s_left)
-        if k in (0, 1):
-            go(at, at, S_W, agf.at[k], to_s_right)
-        pass_on(k, s_left)
-        at = piece(m4(f + k), s_right)
-        got(at, ag2r.at[k], to_s_right)
-        if k == 3:
-            go(at, at, S_W, agf.at[k], to_s_left)
-        pass_on(k, s_right)
-
-    def across(k):
-        got(piece(m4(f + k), opposite), agf.at[k], to_opposite)
-        pass_on(k, opposite)
-
     chunk(0)
-    first_axis(1)
-    first_axis(3)
+    for n in (1, 2):
+        got(piece(n, 0)[0], ag1.at[n - 1], partner)
+        spread(n)
+        along_z(n, 0)
+        pass_on(n, 0)
+
+    def beside(n, m):
+        at, _ = piece(n, m)
+        got(at, ag2.at[4 * n + m], s_devs[m])
+        if m == (3, 1, 3)[n]:
+            go(at, at, S_W, ag2.at[4 * n + 2], s_devs[4 - m])
+        along_z(n, m)
+        pass_on(n, m)
+
     chunk(1)
-    second_axis(0)
-    first_axis(2)
-    second_axis(1)
-    second_axis(3)
+    beside(0, 3)
+    beside(0, 1)
     chunk(2)
-    second_axis(2)
+    beside(1, 1)
+    beside(1, 3)
+    beside(2, 3)
+    beside(2, 1)
     chunk(3)
-    across(0)
+    beside(0, 2)
+    beside(1, 2)
+    beside(2, 2)
+
+    def from_z(n, m):
+        got(piece(n, m, 1)[0], agzz.at[4 * (n - 1) + m], down if n == 1 and m != 2 else up)
+        pass_on(n, m, 1)
+
+    for m in (0, 3, 1):
+        from_z(1, m)
+        from_z(2, m)
 
     far = pl.ds(4 - half, 4)
     rows2 = 256
@@ -293,11 +299,10 @@
     block(0)
     g_recv[me] = g_send[0]
 
-    across(1)
-    across(3)
-    across(2)
-
-    got(r1, rs1, to_right)
+    from_z(1, 2)
+    from_z(2, 2)
+
+    got(r1, rs1, partner)
     for i in range(NY):
         dx, dy = xy(f, i)
         for dz in range(NZH):
@@ -307,12 +312,11 @@
     for k in (1, 3, 2):
         go(u.at[m4(s + k)], u_recv.at[3 - k], S_RS2, rs2, dev_fs(f, m4(s + k)))
 
-
     block(2)
     block(1)
     block(3)
 
-    got(u_recv, rs2, to_s_left)
+    got(u_recv, rs2, partner)
     for dz in range(NZH):
         v[dz] = (u[s, dz] + u_recv[0, dz]) + (u_recv[1, dz] + u_recv[2, dz])
 
@@ -455,7 +459,9 @@
         dma((7,)),
         dma((10,)),
         dma((4,)),
-        dma((4,)), dma((4,)), dma((4,)), dma((4,)),
+        dma((2,)),
+        dma((12,)),
+        dma((8,)),
         dma((NX,)),
         dma((2 * NX,)),
         dma((2 * NX,)),

time: 58 us -> 56.2 us (0.969)
  Pallas kernels: 57.2 us -> 55.3 us
    pallas_call x1, Pallas kernels: 55.3 us -> 53.3 us  [local(): pl.pallas_call(kernel, out_shape=(pltpu.VMEM((tokens, model), BF16), pltp...]
where the time goes in v4:
time: 56.2 us; the launch traced here: 55.9 us
  Pallas kernels  55.3 us (98%)
  between operations  0.64 us (1%)
    pallas_call x1, Pallas kernels, local(): pl.pallas_call(kernel, out_shape=(pltpu.VMEM((tokens, model), BF16), pltp...  53.3 us
    pallas_call x1, Pallas kernels, local(): pl.pallas_call(finish, out_shape=(jax.ShapeDtypeStruct((tokens, model), B...  1.95 us

profile of v4, /device:TPU:1, one launch (start us, length us, event | category | flops | bytes accessed | tf_op | source)
XLA Modules:
  0.0 55.9 jit_solution(12302506993846810547)
XLA Ops:
  0.6 53.3 %shard_map.67 = (bf16[512,2048]{1,0:T(8,128)(2,1)S(1)}, f32[32,128]{1,0:T(8,128)S(1)}) custom-call(bf16[512,2048]{1,0:T(8,128)(2,1)} %act_hbm.1, f32[1,2048]{1,0:T(1,128)} %bitcast.5, bf16[4,16,768]{2,1,0:T(8,128)(2,1)} %bitcast.4, bf16[512,768]{1,0:T(8,128)(2,1)} %grads_hbm.1), custom_call_target="tpu_custom_call" | custom-call | tf_op jit(solution)/shard_map/pallas_call | solution.py:477
  54.0 1.9 %shard_map.68 = (bf16[512,2048]{1,0:T(8,128)(2,1)}, f32[48,64]{1,0:T(8,128)}, f32[1,64]{1,0:T(1,128)}) custom-call(bf16[512,2048]{1,0:T(8,128)(2,1)S(1)} %get-tuple-element.8.raw, f32[32,128]{1,0:T(8,128)S(1)} %get-tuple-element.9.tail), custom_call_target="tpu_custom_call" | custom-call | tf_op jit(solution)/shard_map/pallas_call | solution.py:490

commit v5 on v4

--- a/solution.py
+++ b/solution.py
@@ -244,13 +244,13 @@
     chunk(1)
     beside(0, 3)
     beside(0, 1)
-    chunk(2)
     beside(1, 1)
     beside(1, 3)
     beside(2, 3)
     beside(2, 1)
+    chunk(2)
+    beside(0, 2)
     chunk(3)
-    beside(0, 2)
     beside(1, 2)
     beside(2, 2)
 
@@ -412,15 +412,21 @@
 
 
 def finish(raw, tail, out, weight_grads, gain_grads, buf, come, leave):
-    away = pltpu.make_async_copy(raw, out, leave)
-    away.start()
+    rows = raw.shape[0] // leave.shape[0]
+    away = [
+        pltpu.make_async_copy(raw.at[pl.ds(i * rows, rows)], out.at[pl.ds(i * rows, rows)], leave.at[i])
+        for i in range(leave.shape[0])
+    ]
+    for made in away:
+        made.start()
     into = pltpu.make_async_copy(tail, buf, come)
     into.start()
     into.wait()
     weight_grads[0:24] = buf[0:24, 0:64]
     weight_grads[24:48] = buf[0:24, 64:128]
     gain_grads[...] = buf[24:25, 0:64]
-    away.wait()
+    for made in away:
+        made.wait()
 
 
 def local(activations, norm_gain, key_weight, key_grads):
@@ -496,7 +502,7 @@
         ),
         in_specs=[hbm, hbm],
         out_specs=(hbm, vmem, vmem),
-        scratch_shapes=[pltpu.VMEM((32, 128), F32), dma, dma],
+        scratch_shapes=[pltpu.VMEM((32, 128), F32), dma, dma((4,))],
         compiler_params=pltpu.CompilerParams(vmem_limit_bytes=1024 * 1024),
     )(raw, tail)
     return input_grads, weight_grads.T, gain_grads[0]

time: 56.2 us -> 55.9 us (level)
  no operation moved by 1% of the time
where the time goes in v5:
time: 55.9 us; the launch traced here: 55.7 us
  Pallas kernels  55.1 us (99%)
  between operations  0.64 us (1%)
    pallas_call x1, Pallas kernels, local(): pl.pallas_call(kernel, out_shape=(pltpu.VMEM((tokens, model), BF16), pltp...  53.1 us
    pallas_call x1, Pallas kernels, local(): pl.pallas_call(finish, out_shape=(jax.ShapeDtypeStruct((tokens, model), B...  1.97 us

profile of v5, /device:TPU:1, one launch (start us, length us, event | category | flops | bytes accessed | tf_op | source)
XLA Modules:
  0.0 55.7 jit_solution(14832849790689471540)
XLA Ops:
  0.6 53.1 %shard_map.67 = (bf16[512,2048]{1,0:T(8,128)(2,1)S(1)}, f32[32,128]{1,0:T(8,128)S(1)}) custom-call(bf16[512,2048]{1,0:T(8,128)(2,1)} %act_hbm.1, f32[1,2048]{1,0:T(1,128)} %bitcast.5, bf16[4,16,768]{2,1,0:T(8,128)(2,1)} %bitcast.4, bf16[512,768]{1,0:T(8,128)(2,1)} %grads_hbm.1), custom_call_target="tpu_custom_call" | custom-call | tf_op jit(solution)/shard_map/pallas_call | solution.py:483
  53.8 2.0 %shard_map.68 = (bf16[512,2048]{1,0:T(8,128)(2,1)}, f32[48,64]{1,0:T(8,128)}, f32[1,64]{1,0:T(1,128)}) custom-call(bf16[512,2048]{1,0:T(8,128)(2,1)S(1)} %get-tuple-element.8.raw, f32[32,128]{1,0:T(8,128)S(1)} %get-tuple-element.9.tail), custom_call_target="tpu_custom_call" | custom-call | tf_op jit(solution)/shard_map/pallas_call | solution.py:496
